TPU v7x, 256 devices: a whole 4x4x8 slice. The times are simulated.
256 devices in a mesh: fsdp: 32 (over y_hi, z, core), grp: 8 (over y_lo, x).
Axes of the slice: x: 4, y: 4 (y_hi: 2, y_lo: 2; y = y_hi * 2 + y_lo), z: 8, core: 2. Of those that a mesh axis runs over, the one named last changes fastest.
Arguments:
- hidden_act: bfloat16 [8, 2048, 14336], P('grp', None, 'fsdp'), may hold values from -6 to 6
- grad_output: bfloat16 [8, 2048, 4096], P('grp', 'fsdp'), may hold values from -6 to 6
- down_weight: bfloat16 [14336, 4096], P('fsdp'), may hold values from -0.09375 to 0.09375
- proj_in: bfloat16 [14336, 64], P('fsdp'), may hold values from -0.046875 to 0.046875
- proj_out: bfloat16 [4096, 64], replicated, may hold values from -0.09375 to 0.09375
- example_ids: int32 [8, 2048], P('grp'), may hold values from 0 to 7, never falling along the last dimension, each value on 1 to 512 neighbouring positions
Outputs:
- grad_hidden: bfloat16 [8, 2048, 14336], P('grp', None, 'fsdp')
- gram: float32 [4096, 4096], P('grp', 'fsdp')
- scores: float32 [64], replicated
Inputs may be any that keep to these rules, and one draw needn't show every extreme that they name: `example_ids`: never falls along a group's tokens; each of the 8 examples of a group has 1 to 512 tokens, one exactly 512.
All inputs are finite; a program needn't handle non-finite values.
Results may differ from a plain program's by a relative error of at most 0.001.
Values may be sent and summed in bfloat16 or wider, within the bound.
No kernel may reach another device: no remote copies, remote signals or barrier semaphores. Data moves between devices by JAX's collectives and lax.ppermute only.
A program may use at most 128 MiB of HBM per device.

v0:
```python
import jax
import jax.numpy as jnp
from jax import lax
from jax.sharding import PartitionSpec as P

PROJ = 64
TOK_GRP = 2048
EX_GRP = 8


def inverse_diagonal(matrix):
    lower = jnp.linalg.cholesky(matrix)
    eye = jnp.eye(matrix.shape[0], dtype=matrix.dtype)
    lower_inv = jax.scipy.linalg.solve_triangular(lower, eye, lower=True)
    return jnp.sum(lower_inv * lower_inv, axis=0)


def example_features(ids, left, right):
    onehot = (jnp.arange(EX_GRP, dtype=jnp.int32)[:, None] == ids[None, :]).astype(jnp.float32)
    weighted = (onehot[:, None, :] * jnp.transpose(left)[None, :, :]).reshape(
        EX_GRP * PROJ, ids.shape[0]
    )
    product = jnp.dot(weighted, right, precision=lax.Precision.HIGHEST)
    return product.reshape(EX_GRP, PROJ * PROJ) * (EX_GRP / TOK_GRP) ** 0.5


def body(hidden_act, grad_output, down_weight, proj_in, proj_out, example_ids):
    fsdp_count = lax.axis_size("fsdp")
    group_count = lax.axis_size("grp")
    hidden_rows = hidden_act[0]
    grad_rows = grad_output[0]
    group_ids = example_ids[0]
    tok_rows = grad_rows.shape[0]
    feat_width = PROJ * PROJ
    examples = EX_GRP * group_count
    grad_full = lax.all_gather(grad_rows, "fsdp", axis=0, tiled=True)
    grad_hidden = lax.dot_general(
        grad_full, down_weight, (((1,), (1,)), ((), ())), preferred_element_type=jnp.float32
    )
    grad_hidden = grad_hidden.astype(jnp.bfloat16)[None]
    rows_part = hidden_rows
    left = lax.psum_scatter(
        jnp.dot(rows_part, proj_in, preferred_element_type=jnp.float32),
        "fsdp",
        scatter_dimension=0,
        tiled=True,
    )
    right = jnp.dot(grad_rows, proj_out, preferred_element_type=jnp.float32)
    my_ids = lax.dynamic_slice_in_dim(group_ids, lax.axis_index("fsdp") * tok_rows, tok_rows, 0)
    partial_feats = example_features(my_ids, left, right)
    col_count = feat_width // fsdp_count
    group_feats = lax.psum(partial_feats, "fsdp")
    all_feats = lax.all_gather(group_feats.astype(jnp.bfloat16), "grp", axis=0, tiled=True).astype(
        group_feats.dtype
    )
    own_cols = lax.dynamic_slice_in_dim(
        group_feats, lax.axis_index("fsdp") * col_count, col_count, 1
    )
    rows_part = group_feats
    product = lax.dot_general(
        rows_part,
        own_cols,
        (((0,), (0,)), ((), ())),
        precision=lax.Precision.HIGHEST,
        preferred_element_type=jnp.float32,
    )
    gram = lax.psum_scatter(product / examples, "grp", scatter_dimension=0, tiled=True)
    kernel = lax.dot_general(
        all_feats,
        all_feats,
        (((1,), (1,)), ((), ())),
        precision=lax.Precision.HIGHEST,
        preferred_element_type=jnp.float32,
    )
    ridge = jnp.trace(kernel) / examples
    eye = jnp.eye(examples, dtype=jnp.float32)
    scores = 1.0 - ridge * inverse_diagonal(kernel + ridge * eye)
    return (grad_hidden, gram, scores)


def solution(mesh):
    in_specs = (
        P("grp", None, "fsdp"),
        P("grp", "fsdp", None),
        P("fsdp", None),
        P("fsdp", None),
        P(),
        P("grp", None),
    )
    out_specs = (P("grp", None, "fsdp"), P("grp", "fsdp"), P())
    return jax.shard_map(body, mesh=mesh, in_specs=in_specs, out_specs=out_specs, check_vma=False)
```

profile of v0, /device:TPU:32, one launch (start us, length us, event | category | flops | bytes accessed | tf_op | source)
XLA Modules:
  0.0 566.4 jit_solution(12416813345016848578)
XLA Ops:
  7.2 0.0 copy-start
  7.2 0.0 reduce-scatter.3.cloned.1.call-start
  7.2 1.4 copy-done
  8.7 2.6 fusion.8
  11.3 0.0 reduce-scatter.3.cloned.1.call-update
  11.3 0.0 all-reduce.2.cloned.1.call-start
  11.3 0.7 dynamic-slice_bitcast_fusion
  12.1 0.3 fusion.11
  12.4 117.4 %reduce-scatter.3.cloned.1.call-done = f32[64,64]{1,0:T(8,128)} async-done(((f32[2048,64]{1,0:T(8,128)}), f32[64,64]{1,0:T(8,128)}) %reduce-scatter.3.cloned.1.call-update) | async-done | bytes 16400 | tf_op jit(solution)/shard_map/reduce_scatter | solution.py:42
  129.8 0.8 copy.11
  130.7 0.4 convolution_multiply_fusion.1
  131.1 0.1 copy.12
  131.2 0.8 mul.56
  132.0 0.0 all-reduce.2.cloned.1.call-update
  132.0 0.0 all-gather.3.cloned.1.call-start
  132.1 0.7 all-gather.3.cloned.1.call-update
  132.8 0.0 reduce-scatter.5.cloned.1.call-start
  132.8 239.1 %all-reduce.2.cloned.1.call-done = f32[8,4096]{1,0:T(8,128)} async-done(((f32[8,4096]{1,0:T(8,128)}), f32[8,4096]{1,0:T(8,128)}) %all-reduce.2.cloned.1.call-update) | async-done | bytes 131088 | tf_op jit(solution)/shard_map/psum | solution.py:52
  371.9 5.8 %convolution_multiply_fusion = f32[4096,128]{1,0:T(8,128)} fusion(f32[8,4096]{1,0:T(8,128)} %all-reduce.2.cloned.1.call-done, s32[]{:T(128)S(6)} %select_n.16), kind=kOutput, calls=%fused_computation.2 | convolution fusion | flops 50855936 | bytes 2232324 | tf_op jit(solution)/shard_map/dot_general | solution.py:60
  377.7 0.0 reduce-scatter.5.cloned.1.call-update
  377.7 29.4 %all_gather.7 = bf16[64,4096]{1,0:T(8,128)(2,1)S(1)} all-gather(bf16[8,4096]{1,0:T(8,128)(2,1)S(1)} %convert_element_type.18), channel_id=1, replica_groups=mesh['fsdp'=32,'grp'=8] {'grp'}, dimensions={0}, use_global_device_ids=true | all-gather | bytes 589824 | tf_op jit(solution)/shard_map/all_gather | solution.py:53
  407.1 0.9 select_reduce_fusion.1
  408.0 0.1 copy.13
  408.7 5.8 %cholesky.13 = f32[64,64]{1,0:T(8,128)S(1)} custom-call(f32[64,64]{1,0:T(8,128)S(1)} %fusion.16), custom_call_target="Cholesky" | custom-call | tf_op jit(solution)/shard_map/jit(cholesky)/cholesky | solution.py:12
  414.6 0.6 compare_reduce_fusion
  415.3 0.7 fusion.13
  415.9 4.9 custom-call.7
  420.8 0.2 fusion.10
  421.1 0.5 multiply_subtract_fusion
  421.6 91.2 %all-gather.3.cloned.1.call-done = bf16[1,2048,4096]{2,1,0:T(8,128)(2,1)} async-done(((bf16[1,64,4096]{2,1,0:T(8,128)(2,1)}), bf16[1,2048,4096]{2,1,0:T(8,128)(2,1)}) %all-gather.3.cloned.1.call-update) | async-done | bytes 16777232 | tf_op jit(solution)/shard_map/all_gather | solution.py:36
  512.8 13.3 %fusion.5 = bf16[1,2048,448]{1,2,0:T(8,128)(2,1)} fusion(bf16[448,4096]{1,0:T(8,128)(2,1)} %param.8, bf16[1,2048,4096]{2,1,0:T(8,128)(2,1)} %all-gather.3.cloned.1.call-done), kind=kOutput, calls=%fused_computation.4 | convolution fusion | flops 7517110272 | bytes 22282240 | tf_op jit(solution)/shard_map/dot_general | solution.py:37
  526.2 33.7 %reduce-scatter.5.cloned.1.call-done = f32[512,128]{1,0:T(8,128)} async-done(((f32[4096,128]{1,0:T(8,128)}), f32[512,128]{1,0:T(8,128)}) %reduce-scatter.5.cloned.1.call-update) | async-done | bytes 262160 | tf_op jit(solution)/shard_map/reduce_scatter | solution.py:67
  (11 shorter events, 0.1 us)
Async XLA Ops:
  7.2 1.5 copy-start
  7.2 4.9 copy-start.1
  7.2 4.9 copy-start.3
  7.2 122.6 %reduce-scatter.3.cloned.1.call-start = ((), (), s32[]{:S(2)}) async-start(), calls=%async_computation.2 | async-start | bytes 1081344 | tf_op jit(solution)/shard_map/reduce_scatter | solution.py:42
  11.3 360.6 %all-reduce.2.cloned.1.call-start = ((), (), s32[]{:S(2)}) async-start(), calls=%async_computation.3 | async-start | bytes 262144 | tf_op jit(solution)/shard_map/psum | solution.py:52
  132.0 380.8 %all-gather.3.cloned.1.call-start = ((), (), s32[]{:S(2)}) async-start(), calls=%async_computation.5 | async-start | bytes 17301504 | tf_op jit(solution)/shard_map/all_gather | solution.py:36
  132.8 427.1 %reduce-scatter.5.cloned.1.call-start = ((), (), s32[]{:S(2)}) async-start(), calls=%async_computation.4 | async-start | bytes 2359296 | tf_op jit(solution)/shard_map/reduce_scatter | solution.py:67
  371.9 5.8 %copy-start.2 = (f32[8,4096]{1,0:T(8,128)S(1)}, f32[8,4096]{1,0:T(8,128)}, u32[]{:S(2)}) copy-start(f32[8,4096]{1,0:T(8,128)} %all-reduce.2.cloned.1.call-done) | copy-start | bytes 393220
Sparse Core Ops, SparseCore 0:
  12.7 117.0 reduce-scatter.2
  133.2 238.6 all-reduce.1
  374.7 138.1 all-gather.2
  515.8 43.9 reduce-scatter.4
where the time goes:
time: 567 us; the launch traced here: 566 us
  waiting for transfers between devices  482 us (85%)
  blocking collectives  29.4 us (5%)
  matrix products  23.5 us (4%)
  between operations  14.5 us (3%)
  other arithmetic  12.6 us (2%)
    psum x1, waiting for transfers between devices, body(): group_feats = lax.psum(partial_feats, 'fsdp')  239 us
    reduce_scatter x1, waiting for transfers between devices, body(): lax.psum_scatter(jnp.dot(rows_part, proj_in, preferred_element_type=jnp.f...  117 us
    all_gather x1, waiting for transfers between devices, body(): grad_full = lax.all_gather(grad_rows, 'fsdp', axis=0, tiled=True)  91.2 us
    reduce_scatter x1, waiting for transfers between devices, body(): lax.psum_scatter(product / examples, 'grp', scatter_dimension=0, tiled=True)  33.7 us
    all_gather x1, blocking collectives, body(): lax.all_gather(group_feats.astype(jnp.bfloat16), 'grp', axis=0, tiled=True)  29.4 us
    dot_general x1, matrix products, body(): lax.dot_general(grad_full, down_weight, (((1,), (1,)), ((), ())), preferr...  13.3 us
  transfers between devices with their start and end apart: 4, of which 4 were waited for; matrix products, arithmetic and copies ran while one was open for 6% of the time, Pallas kernels for 0%

commit v1 on v0

--- a/solution.py
+++ b/solution.py
@@ -6,6 +6,12 @@
 PROJ = 64
 TOK_GRP = 2048
 EX_GRP = 8
+
+
+def add_all(x, axis):
+    parts = lax.all_gather(x, axis, axis=0, tiled=False)
+    total = parts.sum(axis=0)
+    return total
 
 
 def inverse_diagonal(matrix):
@@ -49,7 +55,7 @@
     my_ids = lax.dynamic_slice_in_dim(group_ids, lax.axis_index("fsdp") * tok_rows, tok_rows, 0)
     partial_feats = example_features(my_ids, left, right)
     col_count = feat_width // fsdp_count
-    group_feats = lax.psum(partial_feats, "fsdp")
+    group_feats = add_all(partial_feats, "fsdp")
     all_feats = lax.all_gather(group_feats.astype(jnp.bfloat16), "grp", axis=0, tiled=True).astype(
         group_feats.dtype
     )

time: 567 us -> 410 us (0.72)
  waiting for transfers between devices: 482 us -> 325 us
    psum x1 -> x0, waiting for transfers between devices: 239 us -> none  [body(): group_feats = lax.psum(partial_feats, 'fsdp')]
    all_gather x0 -> x1, waiting for transfers between devices: none -> 85.8 us  [add_all(): parts = lax.all_gather(x, axis, axis=0, tiled=False)]
  transfers between devices with their start and end apart: 4 -> 4, of which waited for: 4 -> 4; matrix products, arithmetic and copies ran while one was open for 6% -> 9% of each run, Pallas kernels for 0% -> 0%
where the time goes in v1:
time: 410 us
  waiting for transfers between devices  325 us (79%)
  blocking collectives  29.1 us (7%)
  matrix products  22.5 us (5%)
  other arithmetic  15 us (4%)
  between operations  14.5 us (4%)
    reduce_scatter x1, waiting for transfers between devices, body(): lax.psum_scatter(jnp.dot(rows_part, proj_in, preferred_element_type=jnp.f...  117 us
    all_gather x1, waiting for transfers between devices, body(): grad_full = lax.all_gather(grad_rows, 'fsdp', axis=0, tiled=True)  87 us
    all_gather x1, waiting for transfers between devices, add_all(): parts = lax.all_gather(x, axis, axis=0, tiled=False)  85.8 us
    reduce_scatter x1, waiting for transfers between devices, body(): lax.psum_scatter(product / examples, 'grp', scatter_dimension=0, tiled=True)  33.7 us
    all_gather x1, blocking collectives, body(): lax.all_gather(group_feats.astype(jnp.bfloat16), 'grp', axis=0, tiled=True)  29.1 us
    dot_general x1, matrix products, body(): lax.dot_general(grad_full, down_weight, (((1,), (1,)), ((), ())), preferr...  13.3 us
  transfers between devices with their start and end apart: 4, of which 4 were waited for; matrix products, arithmetic and copies ran while one was open for 9% of the time, Pallas kernels for 0%

profile of v1, /device:TPU:32, one launch (start us, length us, event | category | flops | bytes accessed | tf_op | source)
XLA Modules:
  0.0 410.0 jit_solution(5372258330692015725)
XLA Ops:
  7.2 0.0 reduce-scatter.3.cloned.1.call-start
  7.2 1.4 copy-done
  8.7 2.6 fusion.8
  11.3 0.0 reduce-scatter.3.cloned.1.call-update
  11.3 0.0 all-gather.4.cloned.1.call-start
  11.3 0.7 dynamic-slice_bitcast_fusion
  12.1 0.3 fusion.11
  12.4 117.4 %reduce-scatter.3.cloned.1.call-done = f32[64,64]{1,0:T(8,128)} async-done(((f32[2048,64]{1,0:T(8,128)}), f32[64,64]{1,0:T(8,128)}) %reduce-scatter.3.cloned.1.call-update) | async-done | bytes 16400 | tf_op jit(solution)/shard_map/reduce_scatter | solution.py:48
  129.8 0.8 copy.14
  130.7 0.4 convolution_multiply_fusion.1
  131.1 0.1 copy.15
  131.2 0.8 mul.63
  132.0 0.0 all-gather.4.cloned.1.call-update
  132.0 0.0 all-gather.6.cloned.1.call-start
  132.1 0.7 all-gather.6.cloned.1.call-update
  132.8 0.0 reduce-scatter.5.cloned.1.call-start
  132.8 85.8 %all-gather.4.cloned.1.call-done = f32[32,8,4096]{2,1,0:T(8,128)} async-done(((f32[1,8,4096]{2,1,0:T(8,128)}), f32[32,8,4096]{2,1,0:T(8,128)}) %all-gather.4.cloned.1.call-update) | async-done | bytes 4194320 | tf_op jit(solution)/shard_map/all_gather | solution.py:12
  218.6 2.4 reduce_sum.28
  221.0 4.8 %convolution_multiply_fusion = f32[4096,128]{1,0:T(8,128)} fusion(f32[8,4096]{1,0:T(8,128)S(1)} %reduce_sum.28, s32[]{:T(128)S(6)} %select_n.16), kind=kOutput, calls=%fused_computation.2 | convolution fusion | flops 50855936 | bytes 2232324 | tf_op jit(solution)/shard_map/dot_general | solution.py:66
  225.8 0.0 reduce-scatter.5.cloned.1.call-update
  225.9 29.1 %all_gather.12 = bf16[64,4096]{1,0:T(8,128)(2,1)S(1)} all-gather(bf16[8,4096]{1,0:T(8,128)(2,1)S(1)} %convert_element_type.18), channel_id=1, replica_groups=mesh['fsdp'=32,'grp'=8] {'grp'}, dimensions={0}, use_global_device_ids=true | all-gather | bytes 589824 | tf_op jit(solution)/shard_map/all_gather | solution.py:59
  254.9 0.9 select_reduce_fusion.1
  255.8 0.1 copy.16
  256.6 5.8 %cholesky.13 = f32[64,64]{1,0:T(8,128)S(1)} custom-call(f32[64,64]{1,0:T(8,128)S(1)} %fusion.16), custom_call_target="Cholesky" | custom-call | tf_op jit(solution)/shard_map/jit(cholesky)/cholesky | solution.py:18
  262.5 0.6 compare_reduce_fusion
  263.1 0.7 fusion.13
  263.8 4.9 %custom-call.7 = f32[1,64,64]{1,2,0:T(8,128)S(1)} custom-call(f32[1,64,64]{2,1,0:T(8,128)S(1)} %fusion.13), custom_call_target="InvertDiagBlocksLowerTriangular" | custom-call | tf_op jit(solution)/shard_map/jit(_solve_triangular)/triangular_solve | solution.py:20
  268.7 0.2 fusion.10
  268.9 0.5 multiply_subtract_fusion
  269.4 87.0 %all-gather.6.cloned.1.call-done = bf16[1,2048,4096]{2,1,0:T(8,128)(2,1)} async-done(((bf16[1,64,4096]{2,1,0:T(8,128)(2,1)}), bf16[1,2048,4096]{2,1,0:T(8,128)(2,1)}) %all-gather.6.cloned.1.call-update) | async-done | bytes 16777232 | tf_op jit(solution)/shard_map/all_gather | solution.py:42
  356.5 13.3 %fusion.5 = bf16[1,2048,448]{1,2,0:T(8,128)(2,1)} fusion(bf16[448,4096]{1,0:T(8,128)(2,1)} %param.8, bf16[1,2048,4096]{2,1,0:T(8,128)(2,1)} %all-gather.6.cloned.1.call-done), kind=kOutput, calls=%fused_computation.4 | convolution fusion | flops 7517110272 | bytes 22282240 | tf_op jit(solution)/shard_map/dot_general | solution.py:43
  369.8 33.7 %reduce-scatter.5.cloned.1.call-done = f32[512,128]{1,0:T(8,128)} async-done(((f32[4096,128]{1,0:T(8,128)}), f32[512,128]{1,0:T(8,128)}) %reduce-scatter.5.cloned.1.call-update) | async-done | bytes 262160 | tf_op jit(solution)/shard_map/reduce_scatter | solution.py:73
  (10 shorter events, 0.1 us)
Async XLA Ops:
  7.2 1.5 copy-start
  7.2 4.9 %copy-start.1 = (bf16[1,64,4096]{2,1,0:T(8,128)(2,1)S(1)}, bf16[1,64,4096]{2,1,0:T(8,128)(2,1)}, u32[]{:S(2)}) copy-start(bf16[1,64,4096]{2,1,0:T(8,128)(2,1)} %param.7) | copy-start | bytes 1572868
  7.2 4.9 %copy-start.2 = (bf16[4096,64]{0,1:T(8,128)(2,1)S(1)}, bf16[4096,64]{0,1:T(8,128)(2,1)}, u32[]{:S(2)}) copy-start(bf16[4096,64]{0,1:T(8,128)(2,1)} %param.10) | copy-start | bytes 1572868
  7.2 122.6 %reduce-scatter.3.cloned.1.call-start = ((), (), s32[]{:S(2)}) async-start(), calls=%async_computation.2 | async-start | bytes 1081344 | tf_op jit(solution)/shard_map/reduce_scatter | solution.py:48
  11.3 207.3 %all-gather.4.cloned.1.call-start = ((), (), s32[]{:S(2)}) async-start(), calls=%async_computation.3 | async-start | bytes 4325376 | tf_op jit(solution)/shard_map/all_gather | solution.py:12
  132.0 224.4 %all-gather.6.cloned.1.call-start = ((), (), s32[]{:S(2)}) async-start(), calls=%async_computation.5 | async-start | bytes 17301504 | tf_op jit(solution)/shard_map/all_gather | solution.py:42
  132.8 270.7 %reduce-scatter.5.cloned.1.call-start = ((), (), s32[]{:S(2)}) async-start(), calls=%async_computation.4 | async-start | bytes 2359296 | tf_op jit(solution)/shard_map/reduce_scatter | solution.py:73
Sparse Core Ops, SparseCore 0:
  12.7 117.0 reduce-scatter.2
  133.5 85.0 all-gather.3
  221.8 134.6 all-gather.5
  359.6 43.8 reduce-scatter.4
